TPU v7x, 512 devices: a whole 4x4x16 slice. The times are simulated.
512 devices in a mesh: chain: 128 (over z, y, core), seg: 4 (over x).
Axes of the slice: x: 4, y: 4, z: 16, core: 2. Of those that a mesh axis runs over, the one named last changes fastest.
Arguments:
- band_tiles: bfloat16 [128, 1024, 7, 1024], P('chain', None, None, 'seg'), may hold values from -0.009765625 to 0.009765625
- widths: int32 [128], P('chain'), may hold values from 2 to 6, as said below
- warm_start: float32 [131072, 256], P(('chain', 'seg')), may hold values from -4 to 4
- scores: float32 [131072, 64], P(('chain', 'seg')), may hold values from -6 to 6
- penalty: float32 [256], replicated, may hold values from 0.05 to 0.5
Outputs:
- fitted_effects: float32 [131072, 256], P(('chain', 'seg'))
Inputs may be any that keep to these rules, and one draw needn't show every extreme that they name: `widths`: each block uses between 2 and 6 forward tiles; both 2 and 6 occur in every draw.
All inputs are finite; a program needn't handle non-finite values.
Results may differ from a plain program's by a relative error of at most 0.00085.
Values may be sent and summed in bfloat16 or wider, within the bound.
No kernel may reach another device: no remote copies, remote signals or barrier semaphores. Data moves between devices by JAX's collectives and lax.ppermute only.
A program may use at most 64 MiB of HBM per device.

v0:
```python
import jax
import jax.numpy as jnp
from jax import lax
from jax.sharding import PartitionSpec as P

ITERS = 2
step_size = 0.8


def shifted(value, axis, by):
    length = lax.axis_size(axis)
    pairs = [(i, i + by) for i in range(length) if 0 <= i + by < length]
    return lax.ppermute(value, axis, pairs)


def soft_limit(values, limit):
    return jnp.sign(values) * jnp.maximum(jnp.abs(values) - limit, 0.0)


def per_device(band_tiles, widths, warm_start, scores, penalty):
    local_tiles = band_tiles[0]
    block_len = local_tiles.shape[0]
    depth = local_tiles.shape[1]
    strip_len = local_tiles.shape[2]
    flat_tiles = local_tiles.reshape(block_len, depth * strip_len)
    columns = warm_start.shape[1]
    path_len = columns // scores.shape[1]
    target = jnp.tile(scores, (1, path_len))
    offsets = jnp.arange(depth, dtype=jnp.int32)
    live_flags = offsets <= widths[0]
    live_half = live_flags.astype(jnp.bfloat16)
    live_full = live_flags.astype(jnp.float32)
    estimate = warm_start
    for iteration in range(ITERS):
        current = estimate.astype(jnp.bfloat16)
        whole_block = lax.all_gather(current, "seg", axis=0, tiled=True)
        ahead_list = [current] + [
            shifted(current, "chain", -shift_by) for shift_by in range(1, depth)
        ]
        stacked = (jnp.stack(ahead_list) * live_half[:, None, None]).reshape(
            depth * strip_len, columns
        )

        def forward_term(start_row, count, stacked=stacked):
            return jnp.dot(flat_tiles, stacked, preferred_element_type=jnp.float32)

        forward = lax.psum_scatter(
            forward_term(jnp.int32(0), strip_len * lax.axis_size("seg")).astype(jnp.bfloat16),
            "seg",
            scatter_dimension=0,
            tiled=True,
        ).astype(jnp.float32)
        outgoing = lax.dot_general(
            flat_tiles, whole_block, (((0,), (0,)), ((), ())), preferred_element_type=jnp.float32
        )
        outgoing = outgoing.reshape(depth, strip_len, columns) * live_full[:, None, None]
        backward = outgoing[0]
        for shift_by in range(1, depth):
            backward = backward + shifted(
                outgoing[shift_by].astype(jnp.bfloat16), "chain", shift_by
            ).astype(jnp.float32)
        stepped = estimate - step_size * (estimate + (forward + backward) - target)
        estimate = soft_limit(stepped, step_size * penalty)
    return estimate


def solution(mesh):
    in_specs = (
        P("chain", None, None, "seg"),
        P("chain"),
        P(("chain", "seg"), None),
        P(("chain", "seg"), None),
        P(),
    )
    out_specs = P(("chain", "seg"), None)
    return jax.shard_map(
        per_device, mesh=mesh, in_specs=in_specs, out_specs=out_specs, check_vma=False
    )
```

profile of v0, /device:TPU:65, one launch (start us, length us, event | category | flops | bytes accessed | tf_op | source)
XLA Modules:
  0.0 180.1 jit_solution(8785533673903158669)
XLA Ops:
  7.7 2.7 %collective-permute-start.5 = (bf16[256,256]{0,1:T(8,128)(2,1)S(1)}, bf16[256,256]{0,1:T(8,128)(2,1)S(1)}, u32[]{:S(2)}, u32[]{:S(2)}) collective-permute-start(bf16[256,256]{0,1:T(8,128)(2,1)S(1)} %get-tuple-element.10), channel_id=1, source_target_pairs={{24,0},{28,4},{32,8},{36,12},{40,16},{44,20},{48,24},{52,28},{56,3... | collective-permute-start | bytes 393224 | tf_op jit(solution)/shard_map/ppermute | solution.py:13
  10.4 4.9 %collective-permute-start.4 = (bf16[256,256]{0,1:T(8,128)(2,1)S(1)}, bf16[256,256]{0,1:T(8,128)(2,1)S(1)}, u32[]{:S(2)}, u32[]{:S(2)}) collective-permute-start(bf16[256,256]{0,1:T(8,128)(2,1)S(1)} %get-tuple-element.10), channel_id=1, source_target_pairs={{20,0},{24,4},{28,8},{32,12},{36,16},{40,20},{44,24},{48,28},{52,3... | collective-permute-start | bytes 393224 | tf_op jit(solution)/shard_map/ppermute | solution.py:13
  15.3 2.3 %collective-permute-start.3 = (bf16[256,256]{0,1:T(8,128)(2,1)S(1)}, bf16[256,256]{0,1:T(8,128)(2,1)S(1)}, u32[]{:S(2)}, u32[]{:S(2)}) collective-permute-start(bf16[256,256]{0,1:T(8,128)(2,1)S(1)} %get-tuple-element.10), channel_id=1, source_target_pairs={{16,0},{20,4},{24,8},{28,12},{32,16},{36,20},{40,24},{44,28},{48,3... | collective-permute-start | bytes 393224 | tf_op jit(solution)/shard_map/ppermute | solution.py:13
  17.6 2.9 %collective-permute-start.2 = (bf16[256,256]{0,1:T(8,128)(2,1)S(1)}, bf16[256,256]{0,1:T(8,128)(2,1)S(1)}, u32[]{:S(2)}, u32[]{:S(2)}) collective-permute-start(bf16[256,256]{0,1:T(8,128)(2,1)S(1)} %get-tuple-element.10), channel_id=1, source_target_pairs={{12,0},{16,4},{20,8},{24,12},{28,16},{32,20},{36,24},{40,28},{44,3... | collective-permute-start | bytes 393224 | tf_op jit(solution)/shard_map/ppermute | solution.py:13
  20.5 2.0 %collective-permute-start = (bf16[256,256]{0,1:T(8,128)(2,1)S(1)}, bf16[256,256]{0,1:T(8,128)(2,1)S(1)}, u32[]{:S(2)}, u32[]{:S(2)}) collective-permute-start(bf16[256,256]{0,1:T(8,128)(2,1)S(1)} %get-tuple-element.10), channel_id=1, source_target_pairs={{4,0},{8,4},{12,8},{16,12},{20,16},{24,20},{28,24},{32,28},{36,32}... | collective-permute-start | bytes 393224 | tf_op jit(solution)/shard_map/ppermute | solution.py:13
  22.5 10.2 %all_gather.6 = bf16[1024,256]{0,1:T(8,128)(2,1)S(1)} all-gather(bf16[256,256]{0,1:T(8,128)(2,1)S(1)} %get-tuple-element.10), channel_id=1, replica_groups=mesh['chain'=128,'seg'=4] {'seg'}, dimensions={0}, use_global_device_ids=true | all-gather | bytes 655360 | tf_op jit(solution)/shard_map/all_gather | solution.py:36
  33.4 6.1 %copy.14 = bf16[1,1024,7,256]{1,3,2,0:T(8,128)(2,1)} copy(bf16[1,1024,7,256]{3,1,2,0:T(8,128)(2,1)} %param.5) | data formatting | bytes 7340032 | tf_op args[0]
  39.5 8.1 %collective-permute-start.1 = (bf16[256,256]{0,1:T(8,128)(2,1)S(1)}, bf16[256,256]{0,1:T(8,128)(2,1)S(1)}, u32[]{:S(2)}, u32[]{:S(2)}) collective-permute-start(bf16[256,256]{0,1:T(8,128)(2,1)S(1)} %get-tuple-element.10), channel_id=1, source_target_pairs={{8,0},{12,4},{16,8},{20,12},{24,16},{28,20},{32,24},{36,28},{40,32... | collective-permute-start | bytes 393224 | tf_op jit(solution)/shard_map/ppermute | solution.py:13
  47.7 2.9 %collective-permute-done.1 = bf16[256,256]{0,1:T(8,128)(2,1)S(1)} collective-permute-done((bf16[256,256]{0,1:T(8,128)(2,1)S(1)}, bf16[256,256]{0,1:T(8,128)(2,1)S(1)}, u32[]{:S(2)}, u32[]{:S(2)}) %collective-permute-start.1) | collective-permute-done | bytes 131104 | tf_op jit(solution)/shard_map/ppermute | solution.py:13
  51.4 4.0 %fusion.5 = bf16[1024,256]{0,1:T(8,128)(2,1)} fusion(bf16[1792,256]{1,0:T(8,128)(2,1)S(1)} %bitcast.149, bf16[1024,1792]{0,1:T(8,128)(2,1)} %bitcast.145), kind=kOutput, calls=%fused_computation.6 | convolution fusion | flops 939786240 | bytes 5111808 | tf_op jit(solution)/shard_map/dot_general | solution.py:45
  55.5 3.2 %fusion.29 = (bf16[7,256,256]{1,2,0:T(8,128)(2,1)S(1)}, f32[7,256,256]{1,2,0:T(8,128)S(1)}) fusion(f32[7]{0:T(128)S(1)} %compare_convert_fusion, bf16[1024,256]{0,1:T(8,128)(2,1)S(1)} %all_gather.6, bf16[1,1024,7,256]{1,3,2,0:T(8,128)(2,1)} %copy.14), kind=kOutput, calls=%fused_computation.68 | convolution fusion | flops 940441600 | bytes 6946844 | tf_op jit(solution)/shard_map/dot_general | solution.py:53
  58.8 7.5 %collective-permute-start.6 = (bf16[256,256]{0,1:T(8,128)(2,1)S(1)}, bf16[256,256]{0,1:T(8,128)(2,1)S(1)}, u32[]{:S(2)}, u32[]{:S(2)}) collective-permute-start(bf16[256,256]{0,1:T(8,128)(2,1)S(1)} %get-tuple-element.17), channel_id=1, source_target_pairs={{0,4},{4,8},{8,12},{12,16},{16,20},{20,24},{24,28},{28,32},{32,36}... | collective-permute-start | bytes 393224 | tf_op jit(solution)/shard_map/ppermute | solution.py:13
  70.2 4.1 %collective-permute-start.9 = (bf16[256,256]{0,1:T(8,128)(2,1)S(1)}, bf16[256,256]{0,1:T(8,128)(2,1)S(1)}, u32[]{:S(2)}, u32[]{:S(2)}) collective-permute-start(bf16[256,256]{0,1:T(8,128)(2,1)S(1)} %get-tuple-element.20), channel_id=1, source_target_pairs={{0,16},{4,20},{8,24},{12,28},{16,32},{20,36},{24,40},{28,44},{32,4... | collective-permute-start | bytes 393224 | tf_op jit(solution)/shard_map/ppermute | solution.py:13
  74.3 5.4 %collective-permute-start.8 = (bf16[256,256]{0,1:T(8,128)(2,1)S(1)}, bf16[256,256]{0,1:T(8,128)(2,1)S(1)}, u32[]{:S(2)}, u32[]{:S(2)}) collective-permute-start(bf16[256,256]{0,1:T(8,128)(2,1)S(1)} %get-tuple-element.21), channel_id=1, source_target_pairs={{0,12},{4,16},{8,20},{12,24},{16,28},{20,32},{24,36},{28,40},{32,4... | collective-permute-start | bytes 393224 | tf_op jit(solution)/shard_map/ppermute | solution.py:13
  79.6 4.1 %collective-permute-start.7 = (bf16[256,256]{0,1:T(8,128)(2,1)S(1)}, bf16[256,256]{0,1:T(8,128)(2,1)S(1)}, u32[]{:S(2)}, u32[]{:S(2)}) collective-permute-start(bf16[256,256]{0,1:T(8,128)(2,1)S(1)} %get-tuple-element.22), channel_id=1, source_target_pairs={{0,8},{4,12},{8,16},{12,20},{16,24},{20,28},{24,32},{28,36},{32,40... | collective-permute-start | bytes 393224 | tf_op jit(solution)/shard_map/ppermute | solution.py:13
  85.3 3.4 %collective-permute-done.7 = bf16[256,256]{0,1:T(8,128)(2,1)S(1)} collective-permute-done((bf16[256,256]{0,1:T(8,128)(2,1)S(1)}, bf16[256,256]{0,1:T(8,128)(2,1)S(1)}, u32[]{:S(2)}, u32[]{:S(2)}) %collective-permute-start.7) | collective-permute-done | bytes 131104 | tf_op jit(solution)/shard_map/ppermute | solution.py:13
  89.9 2.6 %collective-permute-start.17 = (bf16[256,256]{0,1:T(8,128)(2,1)S(1)}, bf16[256,256]{0,1:T(8,128)(2,1)S(1)}, u32[]{:S(2)}, u32[]{:S(2)}) collective-permute-start(bf16[256,256]{0,1:T(8,128)(2,1)S(1)} %get-tuple-element.6), channel_id=1, source_target_pairs={{24,0},{28,4},{32,8},{36,12},{40,16},{44,20},{48,24},{52,28},{56,3... | collective-permute-start | bytes 393224 | tf_op jit(solution)/shard_map/ppermute | solution.py:13
  92.6 7.3 %collective-permute-start.16 = (bf16[256,256]{0,1:T(8,128)(2,1)S(1)}, bf16[256,256]{0,1:T(8,128)(2,1)S(1)}, u32[]{:S(2)}, u32[]{:S(2)}) collective-permute-start(bf16[256,256]{0,1:T(8,128)(2,1)S(1)} %get-tuple-element.6), channel_id=1, source_target_pairs={{20,0},{24,4},{28,8},{32,12},{36,16},{40,20},{44,24},{48,28},{52,3... | collective-permute-start | bytes 393224 | tf_op jit(solution)/shard_map/ppermute | solution.py:13
  99.9 2.5 %collective-permute-start.15 = (bf16[256,256]{0,1:T(8,128)(2,1)S(1)}, bf16[256,256]{0,1:T(8,128)(2,1)S(1)}, u32[]{:S(2)}, u32[]{:S(2)}) collective-permute-start(bf16[256,256]{0,1:T(8,128)(2,1)S(1)} %get-tuple-element.6), channel_id=1, source_target_pairs={{16,0},{20,4},{24,8},{28,12},{32,16},{36,20},{40,24},{44,28},{48,3... | collective-permute-start | bytes 393224 | tf_op jit(solution)/shard_map/ppermute | solution.py:13
  102.4 2.9 %collective-permute-start.14 = (bf16[256,256]{0,1:T(8,128)(2,1)S(1)}, bf16[256,256]{0,1:T(8,128)(2,1)S(1)}, u32[]{:S(2)}, u32[]{:S(2)}) collective-permute-start(bf16[256,256]{0,1:T(8,128)(2,1)S(1)} %get-tuple-element.6), channel_id=1, source_target_pairs={{12,0},{16,4},{20,8},{24,12},{28,16},{32,20},{36,24},{40,28},{44,3... | collective-permute-start | bytes 393224 | tf_op jit(solution)/shard_map/ppermute | solution.py:13
  105.3 2.0 %collective-permute-start.12 = (bf16[256,256]{0,1:T(8,128)(2,1)S(1)}, bf16[256,256]{0,1:T(8,128)(2,1)S(1)}, u32[]{:S(2)}, u32[]{:S(2)}) collective-permute-start(bf16[256,256]{0,1:T(8,128)(2,1)S(1)} %get-tuple-element.6), channel_id=1, source_target_pairs={{4,0},{8,4},{12,8},{16,12},{20,16},{24,20},{28,24},{32,28},{36,32}... | collective-permute-start | bytes 393224 | tf_op jit(solution)/shard_map/ppermute | solution.py:13
  107.3 9.9 %all_gather.7 = bf16[1024,256]{0,1:T(8,128)(2,1)S(1)} all-gather(bf16[256,256]{0,1:T(8,128)(2,1)S(1)} %get-tuple-element.6), channel_id=1, replica_groups=mesh['chain'=128,'seg'=4] {'seg'}, dimensions={0}, use_global_device_ids=true | all-gather | bytes 655360 | tf_op jit(solution)/shard_map/all_gather | solution.py:36
  117.2 3.2 %collective-permute-start.13 = (bf16[256,256]{0,1:T(8,128)(2,1)S(1)}, bf16[256,256]{0,1:T(8,128)(2,1)S(1)}, u32[]{:S(2)}, u32[]{:S(2)}) collective-permute-start(bf16[256,256]{0,1:T(8,128)(2,1)S(1)} %get-tuple-element.6), channel_id=1, source_target_pairs={{8,0},{12,4},{16,8},{20,12},{24,16},{28,20},{32,24},{36,28},{40,32... | collective-permute-start | bytes 393224 | tf_op jit(solution)/shard_map/ppermute | solution.py:13
  120.5 2.5 %collective-permute-done.13 = bf16[256,256]{0,1:T(8,128)(2,1)S(1)} collective-permute-done((bf16[256,256]{0,1:T(8,128)(2,1)S(1)}, bf16[256,256]{0,1:T(8,128)(2,1)S(1)}, u32[]{:S(2)}, u32[]{:S(2)}) %collective-permute-start.13) | collective-permute-done | bytes 131104 | tf_op jit(solution)/shard_map/ppermute | solution.py:13
  123.8 4.0 %fusion.6 = bf16[1024,256]{0,1:T(8,128)(2,1)} fusion(bf16[1792,256]{1,0:T(8,128)(2,1)S(1)} %bitcast.150, bf16[1024,1792]{0,1:T(8,128)(2,1)} %bitcast.146), kind=kOutput, calls=%fused_computation.7 | convolution fusion | flops 939786240 | bytes 5111808 | tf_op jit(solution)/shard_map/dot_general | solution.py:45
  127.8 3.2 %convolution_bitcast_fusion = f32[1792,256]{0,1:T(8,128)S(1)} fusion(bf16[1024,256]{0,1:T(8,128)(2,1)S(1)} %all_gather.7, bf16[1024,1792]{0,1:T(8,128)(2,1)} %bitcast.147), kind=kOutput, calls=%fused_computation.2 | convolution fusion | flops 939524096 | bytes 6029312 | tf_op jit(solution)/shard_map/dot_general | solution.py:53
  136.2 8.0 %collective-permute-start.18 = (bf16[256,256]{0,1:T(8,128)(2,1)S(1)}, bf16[256,256]{0,1:T(8,128)(2,1)S(1)}, u32[]{:S(2)}, u32[]{:S(2)}) collective-permute-start(bf16[256,256]{0,1:T(8,128)(2,1)S(1)} %get-tuple-element.11), channel_id=1, source_target_pairs={{0,4},{4,8},{8,12},{12,16},{16,20},{20,24},{24,28},{28,32},{32,36}... | collective-permute-start | bytes 393224 | tf_op jit(solution)/shard_map/ppermute | solution.py:13
  144.2 5.8 %collective-permute-start.23 = (bf16[256,256]{0,1:T(8,128)(2,1)S(1)}, bf16[256,256]{0,1:T(8,128)(2,1)S(1)}, u32[]{:S(2)}, u32[]{:S(2)}) collective-permute-start(bf16[256,256]{0,1:T(8,128)(2,1)S(1)} %get-tuple-element.12), channel_id=1, source_target_pairs={{0,24},{4,28},{8,32},{12,36},{16,40},{20,44},{24,48},{28,52},{32,5... | collective-permute-start | bytes 393224 | tf_op jit(solution)/shard_map/ppermute | solution.py:13
  151.9 4.9 %collective-permute-start.21 = (bf16[256,256]{0,1:T(8,128)(2,1)S(1)}, bf16[256,256]{0,1:T(8,128)(2,1)S(1)}, u32[]{:S(2)}, u32[]{:S(2)}) collective-permute-start(bf16[256,256]{0,1:T(8,128)(2,1)S(1)} %get-tuple-element.14), channel_id=1, source_target_pairs={{0,16},{4,20},{8,24},{12,28},{16,32},{20,36},{24,40},{28,44},{32,4... | collective-permute-start | bytes 393224 | tf_op jit(solution)/shard_map/ppermute | solution.py:13
  156.8 5.6 %collective-permute-start.20 = (bf16[256,256]{0,1:T(8,128)(2,1)S(1)}, bf16[256,256]{0,1:T(8,128)(2,1)S(1)}, u32[]{:S(2)}, u32[]{:S(2)}) collective-permute-start(bf16[256,256]{0,1:T(8,128)(2,1)S(1)} %get-tuple-element.15), channel_id=1, source_target_pairs={{0,12},{4,16},{8,20},{12,24},{16,28},{20,32},{24,36},{28,40},{32,4... | collective-permute-start | bytes 393224 | tf_op jit(solution)/shard_map/ppermute | solution.py:13
  162.5 3.8 %collective-permute-start.19 = (bf16[256,256]{0,1:T(8,128)(2,1)S(1)}, bf16[256,256]{0,1:T(8,128)(2,1)S(1)}, u32[]{:S(2)}, u32[]{:S(2)}) collective-permute-start(bf16[256,256]{0,1:T(8,128)(2,1)S(1)} %get-tuple-element.16), channel_id=1, source_target_pairs={{0,8},{4,12},{8,16},{12,20},{16,24},{20,28},{24,32},{28,36},{32,40... | collective-permute-start | bytes 393224 | tf_op jit(solution)/shard_map/ppermute | solution.py:13
  168.1 3.1 %collective-permute-done.19 = bf16[256,256]{0,1:T(8,128)(2,1)S(1)} collective-permute-done((bf16[256,256]{0,1:T(8,128)(2,1)S(1)}, bf16[256,256]{0,1:T(8,128)(2,1)S(1)}, u32[]{:S(2)}, u32[]{:S(2)}) %collective-permute-start.19) | collective-permute-done | bytes 131104 | tf_op jit(solution)/shard_map/ppermute | solution.py:13
  (62 shorter events, 20.4 us)
Async XLA Ops:
  6.5 82.2 %reduce-scatter.3.cloned.1.call-start = ((), (), s32[]{:S(2)}) async-start(), calls=%async_computation.2 | async-start | bytes 655360 | tf_op jit(solution)/shard_map/reduce_scatter | solution.py:47
  7.7 43.0 %collective-permute-start.5 = (bf16[256,256]{0,1:T(8,128)(2,1)S(1)}, bf16[256,256]{0,1:T(8,128)(2,1)S(1)}, u32[]{:S(2)}, u32[]{:S(2)}) collective-permute-start(bf16[256,256]{0,1:T(8,128)(2,1)S(1)} %get-tuple-element.10), channel_id=1, source_target_pairs={{24,0},{28,4},{32,8},{36,12},{40,16},{44,20},{48,24},{52,28},{56,3... | collective-permute-start | bytes 393224 | tf_op jit(solution)/shard_map/ppermute | solution.py:13
  10.4 40.2 %collective-permute-start.4 = (bf16[256,256]{0,1:T(8,128)(2,1)S(1)}, bf16[256,256]{0,1:T(8,128)(2,1)S(1)}, u32[]{:S(2)}, u32[]{:S(2)}) collective-permute-start(bf16[256,256]{0,1:T(8,128)(2,1)S(1)} %get-tuple-element.10), channel_id=1, source_target_pairs={{20,0},{24,4},{28,8},{32,12},{36,16},{40,20},{44,24},{48,28},{52,3... | collective-permute-start | bytes 393224 | tf_op jit(solution)/shard_map/ppermute | solution.py:13
  15.3 35.3 %collective-permute-start.3 = (bf16[256,256]{0,1:T(8,128)(2,1)S(1)}, bf16[256,256]{0,1:T(8,128)(2,1)S(1)}, u32[]{:S(2)}, u32[]{:S(2)}) collective-permute-start(bf16[256,256]{0,1:T(8,128)(2,1)S(1)} %get-tuple-element.10), channel_id=1, source_target_pairs={{16,0},{20,4},{24,8},{28,12},{32,16},{36,20},{40,24},{44,28},{48,3... | collective-permute-start | bytes 393224 | tf_op jit(solution)/shard_map/ppermute | solution.py:13
  17.6 33.0 %collective-permute-start.2 = (bf16[256,256]{0,1:T(8,128)(2,1)S(1)}, bf16[256,256]{0,1:T(8,128)(2,1)S(1)}, u32[]{:S(2)}, u32[]{:S(2)}) collective-permute-start(bf16[256,256]{0,1:T(8,128)(2,1)S(1)} %get-tuple-element.10), channel_id=1, source_target_pairs={{12,0},{16,4},{20,8},{24,12},{28,16},{32,20},{36,24},{40,28},{44,3... | collective-permute-start | bytes 393224 | tf_op jit(solution)/shard_map/ppermute | solution.py:13
  20.5 19.0 %collective-permute-start = (bf16[256,256]{0,1:T(8,128)(2,1)S(1)}, bf16[256,256]{0,1:T(8,128)(2,1)S(1)}, u32[]{:S(2)}, u32[]{:S(2)}) collective-permute-start(bf16[256,256]{0,1:T(8,128)(2,1)S(1)} %get-tuple-element.10), channel_id=1, source_target_pairs={{4,0},{8,4},{12,8},{16,12},{20,16},{24,20},{28,24},{32,28},{36,32}... | collective-permute-start | bytes 393224 | tf_op jit(solution)/shard_map/ppermute | solution.py:13
  39.5 11.0 %collective-permute-start.1 = (bf16[256,256]{0,1:T(8,128)(2,1)S(1)}, bf16[256,256]{0,1:T(8,128)(2,1)S(1)}, u32[]{:S(2)}, u32[]{:S(2)}) collective-permute-start(bf16[256,256]{0,1:T(8,128)(2,1)S(1)} %get-tuple-element.10), channel_id=1, source_target_pairs={{8,0},{12,4},{16,8},{20,12},{24,16},{28,20},{32,24},{36,28},{40,32... | collective-permute-start | bytes 393224 | tf_op jit(solution)/shard_map/ppermute | solution.py:13
  55.4 115.8 %reduce-scatter.5.cloned.1.call-start = ((), (), s32[]{:S(2)}) async-start(), calls=%async_computation.3 | async-start | bytes 655360 | tf_op jit(solution)/shard_map/reduce_scatter | solution.py:47
  55.5 28.3 %copy-start.1 = (f32[256]{0:T(256)S(1)}, f32[256]{0:T(256)}, u32[]{:S(2)}) copy-start(f32[256]{0:T(256)} %param.9) | copy-start | bytes 3076
  55.5 33.2 %copy-start = (f32[256,64]{0,1:T(8,128)S(1)}, f32[256,64]{0,1:T(8,128)}, u32[]{:S(2)}) copy-start(f32[256,64]{0,1:T(8,128)} %param.8) | copy-start | bytes 196612
  58.8 20.8 %collective-permute-start.6 = (bf16[256,256]{0,1:T(8,128)(2,1)S(1)}, bf16[256,256]{0,1:T(8,128)(2,1)S(1)}, u32[]{:S(2)}, u32[]{:S(2)}) collective-permute-start(bf16[256,256]{0,1:T(8,128)(2,1)S(1)} %get-tuple-element.17), channel_id=1, source_target_pairs={{0,4},{4,8},{8,12},{12,16},{16,20},{20,24},{24,28},{28,32},{32,36}... | collective-permute-start | bytes 393224 | tf_op jit(solution)/shard_map/ppermute | solution.py:13
  66.3 17.5 %collective-permute-start.11 = (bf16[256,256]{0,1:T(8,128)(2,1)S(1)}, bf16[256,256]{0,1:T(8,128)(2,1)S(1)}, u32[]{:S(2)}, u32[]{:S(2)}) collective-permute-start(bf16[256,256]{0,1:T(8,128)(2,1)S(1)} %get-tuple-element.18), channel_id=1, source_target_pairs={{0,24},{4,28},{8,32},{12,36},{16,40},{20,44},{24,48},{28,52},{32,5... | collective-permute-start | bytes 393224 | tf_op jit(solution)/shard_map/ppermute | solution.py:13
  68.2 15.6 %collective-permute-start.10 = (bf16[256,256]{0,1:T(8,128)(2,1)S(1)}, bf16[256,256]{0,1:T(8,128)(2,1)S(1)}, u32[]{:S(2)}, u32[]{:S(2)}) collective-permute-start(bf16[256,256]{0,1:T(8,128)(2,1)S(1)} %get-tuple-element.19), channel_id=1, source_target_pairs={{0,20},{4,24},{8,28},{12,32},{16,36},{20,40},{24,44},{28,48},{32,5... | collective-permute-start | bytes 393224 | tf_op jit(solution)/shard_map/ppermute | solution.py:13
  70.2 13.6 %collective-permute-start.9 = (bf16[256,256]{0,1:T(8,128)(2,1)S(1)}, bf16[256,256]{0,1:T(8,128)(2,1)S(1)}, u32[]{:S(2)}, u32[]{:S(2)}) collective-permute-start(bf16[256,256]{0,1:T(8,128)(2,1)S(1)} %get-tuple-element.20), channel_id=1, source_target_pairs={{0,16},{4,20},{8,24},{12,28},{16,32},{20,36},{24,40},{28,44},{32,4... | collective-permute-start | bytes 393224 | tf_op jit(solution)/shard_map/ppermute | solution.py:13
  74.3 11.0 %collective-permute-start.8 = (bf16[256,256]{0,1:T(8,128)(2,1)S(1)}, bf16[256,256]{0,1:T(8,128)(2,1)S(1)}, u32[]{:S(2)}, u32[]{:S(2)}) collective-permute-start(bf16[256,256]{0,1:T(8,128)(2,1)S(1)} %get-tuple-element.21), channel_id=1, source_target_pairs={{0,12},{4,16},{8,20},{12,24},{16,28},{20,32},{24,36},{28,40},{32,4... | collective-permute-start | bytes 393224 | tf_op jit(solution)/shard_map/ppermute | solution.py:13
  79.6 9.1 %collective-permute-start.7 = (bf16[256,256]{0,1:T(8,128)(2,1)S(1)}, bf16[256,256]{0,1:T(8,128)(2,1)S(1)}, u32[]{:S(2)}, u32[]{:S(2)}) collective-permute-start(bf16[256,256]{0,1:T(8,128)(2,1)S(1)} %get-tuple-element.22), channel_id=1, source_target_pairs={{0,8},{4,12},{8,16},{12,20},{16,24},{20,28},{24,32},{28,36},{32,40... | collective-permute-start | bytes 393224 | tf_op jit(solution)/shard_map/ppermute | solution.py:13
  89.9 33.1 %collective-permute-start.17 = (bf16[256,256]{0,1:T(8,128)(2,1)S(1)}, bf16[256,256]{0,1:T(8,128)(2,1)S(1)}, u32[]{:S(2)}, u32[]{:S(2)}) collective-permute-start(bf16[256,256]{0,1:T(8,128)(2,1)S(1)} %get-tuple-element.6), channel_id=1, source_target_pairs={{24,0},{28,4},{32,8},{36,12},{40,16},{44,20},{48,24},{52,28},{56,3... | collective-permute-start | bytes 393224 | tf_op jit(solution)/shard_map/ppermute | solution.py:13
  92.6 30.5 %collective-permute-start.16 = (bf16[256,256]{0,1:T(8,128)(2,1)S(1)}, bf16[256,256]{0,1:T(8,128)(2,1)S(1)}, u32[]{:S(2)}, u32[]{:S(2)}) collective-permute-start(bf16[256,256]{0,1:T(8,128)(2,1)S(1)} %get-tuple-element.6), channel_id=1, source_target_pairs={{20,0},{24,4},{28,8},{32,12},{36,16},{40,20},{44,24},{48,28},{52,3... | collective-permute-start | bytes 393224 | tf_op jit(solution)/shard_map/ppermute | solution.py:13
  99.9 23.1 %collective-permute-start.15 = (bf16[256,256]{0,1:T(8,128)(2,1)S(1)}, bf16[256,256]{0,1:T(8,128)(2,1)S(1)}, u32[]{:S(2)}, u32[]{:S(2)}) collective-permute-start(bf16[256,256]{0,1:T(8,128)(2,1)S(1)} %get-tuple-element.6), channel_id=1, source_target_pairs={{16,0},{20,4},{24,8},{28,12},{32,16},{36,20},{40,24},{44,28},{48,3... | collective-permute-start | bytes 393224 | tf_op jit(solution)/shard_map/ppermute | solution.py:13
  102.4 20.6 %collective-permute-start.14 = (bf16[256,256]{0,1:T(8,128)(2,1)S(1)}, bf16[256,256]{0,1:T(8,128)(2,1)S(1)}, u32[]{:S(2)}, u32[]{:S(2)}) collective-permute-start(bf16[256,256]{0,1:T(8,128)(2,1)S(1)} %get-tuple-element.6), channel_id=1, source_target_pairs={{12,0},{16,4},{20,8},{24,12},{28,16},{32,20},{36,24},{40,28},{44,3... | collective-permute-start | bytes 393224 | tf_op jit(solution)/shard_map/ppermute | solution.py:13
  105.3 11.9 %collective-permute-start.12 = (bf16[256,256]{0,1:T(8,128)(2,1)S(1)}, bf16[256,256]{0,1:T(8,128)(2,1)S(1)}, u32[]{:S(2)}, u32[]{:S(2)}) collective-permute-start(bf16[256,256]{0,1:T(8,128)(2,1)S(1)} %get-tuple-element.6), channel_id=1, source_target_pairs={{4,0},{8,4},{12,8},{16,12},{20,16},{24,20},{28,24},{32,28},{36,32}... | collective-permute-start | bytes 393224 | tf_op jit(solution)/shard_map/ppermute | solution.py:13
  117.2 5.7 %collective-permute-start.13 = (bf16[256,256]{0,1:T(8,128)(2,1)S(1)}, bf16[256,256]{0,1:T(8,128)(2,1)S(1)}, u32[]{:S(2)}, u32[]{:S(2)}) collective-permute-start(bf16[256,256]{0,1:T(8,128)(2,1)S(1)} %get-tuple-element.6), channel_id=1, source_target_pairs={{8,0},{12,4},{16,8},{20,12},{24,16},{28,20},{32,24},{36,28},{40,32... | collective-permute-start | bytes 393224 | tf_op jit(solution)/shard_map/ppermute | solution.py:13
  136.2 26.3 %collective-permute-start.18 = (bf16[256,256]{0,1:T(8,128)(2,1)S(1)}, bf16[256,256]{0,1:T(8,128)(2,1)S(1)}, u32[]{:S(2)}, u32[]{:S(2)}) collective-permute-start(bf16[256,256]{0,1:T(8,128)(2,1)S(1)} %get-tuple-element.11), channel_id=1, source_target_pairs={{0,4},{4,8},{8,12},{12,16},{16,20},{20,24},{24,28},{28,32},{32,36}... | collective-permute-start | bytes 393224 | tf_op jit(solution)/shard_map/ppermute | solution.py:13
  144.2 22.0 %collective-permute-start.23 = (bf16[256,256]{0,1:T(8,128)(2,1)S(1)}, bf16[256,256]{0,1:T(8,128)(2,1)S(1)}, u32[]{:S(2)}, u32[]{:S(2)}) collective-permute-start(bf16[256,256]{0,1:T(8,128)(2,1)S(1)} %get-tuple-element.12), channel_id=1, source_target_pairs={{0,24},{4,28},{8,32},{12,36},{16,40},{20,44},{24,48},{28,52},{32,5... | collective-permute-start | bytes 393224 | tf_op jit(solution)/shard_map/ppermute | solution.py:13
  150.0 16.3 %collective-permute-start.22 = (bf16[256,256]{0,1:T(8,128)(2,1)S(1)}, bf16[256,256]{0,1:T(8,128)(2,1)S(1)}, u32[]{:S(2)}, u32[]{:S(2)}) collective-permute-start(bf16[256,256]{0,1:T(8,128)(2,1)S(1)} %get-tuple-element.13), channel_id=1, source_target_pairs={{0,20},{4,24},{8,28},{12,32},{16,36},{20,40},{24,44},{28,48},{32,5... | collective-permute-start | bytes 393224 | tf_op jit(solution)/shard_map/ppermute | solution.py:13
  151.9 14.3 %collective-permute-start.21 = (bf16[256,256]{0,1:T(8,128)(2,1)S(1)}, bf16[256,256]{0,1:T(8,128)(2,1)S(1)}, u32[]{:S(2)}, u32[]{:S(2)}) collective-permute-start(bf16[256,256]{0,1:T(8,128)(2,1)S(1)} %get-tuple-element.14), channel_id=1, source_target_pairs={{0,16},{4,20},{8,24},{12,28},{16,32},{20,36},{24,40},{28,44},{32,4... | collective-permute-start | bytes 393224 | tf_op jit(solution)/shard_map/ppermute | solution.py:13
  156.8 11.3 %collective-permute-start.20 = (bf16[256,256]{0,1:T(8,128)(2,1)S(1)}, bf16[256,256]{0,1:T(8,128)(2,1)S(1)}, u32[]{:S(2)}, u32[]{:S(2)}) collective-permute-start(bf16[256,256]{0,1:T(8,128)(2,1)S(1)} %get-tuple-element.15), channel_id=1, source_target_pairs={{0,12},{4,16},{8,20},{12,24},{16,28},{20,32},{24,36},{28,40},{32,4... | collective-permute-start | bytes 393224 | tf_op jit(solution)/shard_map/ppermute | solution.py:13
  162.5 8.7 %collective-permute-start.19 = (bf16[256,256]{0,1:T(8,128)(2,1)S(1)}, bf16[256,256]{0,1:T(8,128)(2,1)S(1)}, u32[]{:S(2)}, u32[]{:S(2)}) collective-permute-start(bf16[256,256]{0,1:T(8,128)(2,1)S(1)} %get-tuple-element.16), channel_id=1, source_target_pairs={{0,8},{4,12},{8,16},{12,20},{16,24},{20,28},{24,32},{28,36},{32,40... | collective-permute-start | bytes 393224 | tf_op jit(solution)/shard_map/ppermute | solution.py:13
Sparse Core Ops, SparseCore 0:
  55.6 32.8 reduce-scatter.2
  128.0 33.7 reduce-scatter.4
where the time goes:
time: 181 us; the launch traced here: 180 us
  starting transfers between devices  98.5 us (54%)
  blocking collectives  20.1 us (11%)
  waiting for transfers between devices  15.3 us (8%)
  between operations  14.6 us (8%)
  matrix products  14.4 us (8%)
  local copies, waits for them, and re-layouts  13 us (7%)
  other arithmetic  4.26 us (2%)
    ppermute x24, starting transfers between devices, shifted(): return lax.ppermute(value, axis, pairs)  98.4 us
    all_gather x2, blocking collectives, per_device(): whole_block = lax.all_gather(current, 'seg', axis=0, tiled=True)  20.1 us
    ppermute x24, waiting for transfers between devices, shifted(): return lax.ppermute(value, axis, pairs)  15.3 us
    dot_general x2, matrix products, forward_term(): return jnp.dot(flat_tiles, stacked, preferred_element_type=jnp.float32)  7.95 us
    unnamed x16, local copies, waits for them, and re-layouts  7.27 us
    dot_general x2, matrix products, per_device(): lax.dot_general(flat_tiles, whole_block, (((0,), (0,)), ((), ())), prefer...  6.41 us
  transfers between devices with their start and end apart: 26, of which 6 were waited for; matrix products, arithmetic and copies ran while one was open for 10% of the time, Pallas kernels for 0%

commit v1 on v0

--- a/solution.py
+++ b/solution.py
@@ -1,3 +1,4 @@
+import functools
 import jax
 import jax.numpy as jnp
 from jax import lax
@@ -5,6 +6,15 @@
 
 ITERS = 2
 step_size = 0.8
+
+
+def use_screen(vec, mesh_name):
+    full_n = lax.axis_size(mesh_name)
+    h_now = jnp.tile(vec, [full_n if nth == 0 else 1 for nth in range(vec.ndim)])
+    return lax.all_to_all(h_now, mesh_name, split_axis=0, concat_axis=0, tiled=True)
+
+
+_switch_surface = functools.partial(use_screen, mesh_name="seg")
 
 
 def shifted(value, axis, by):
@@ -33,7 +43,7 @@
     estimate = warm_start
     for iteration in range(ITERS):
         current = estimate.astype(jnp.bfloat16)
-        whole_block = lax.all_gather(current, "seg", axis=0, tiled=True)
+        whole_block = _switch_surface(current)
         ahead_list = [current] + [
             shifted(current, "chain", -shift_by) for shift_by in range(1, depth)
         ]

time: 181 us -> 167 us (0.923)
  the two profiles are of different devices: /device:TPU:65 before, /device:TPU:67 now
where the time goes in v1:
time: 167 us; the launch traced here: 165 us
  starting transfers between devices  97.5 us (58%)
  waiting for transfers between devices  18.5 us (11%)
  local copies, waits for them, and re-layouts  15.6 us (9%)
  between operations  14.7 us (9%)
  matrix products  14.6 us (9%)
  other arithmetic  4.59 us (3%)
    ppermute x24, starting transfers between devices, shifted(): return lax.ppermute(value, axis, pairs)  86.7 us
    ppermute x24, waiting for transfers between devices, shifted(): return lax.ppermute(value, axis, pairs)  18.5 us
    all_to_all x2, starting transfers between devices, use_screen(): lax.all_to_all(h_now, mesh_name, split_axis=0, concat_axis=0, tiled=True)  10.8 us
    dot_general x2, matrix products, forward_term(): return jnp.dot(flat_tiles, stacked, preferred_element_type=jnp.float32)  7.98 us
    unnamed x28, local copies, waits for them, and re-layouts  7.98 us
    dot_general x2, matrix products, per_device(): lax.dot_general(flat_tiles, whole_block, (((0,), (0,)), ((), ())), prefer...  6.6 us
  transfers between devices with their start and end apart: 28, of which 5 were waited for; matrix products, arithmetic and copies ran while one was open for 18% of the time, Pallas kernels for 0%

profile of v1, /device:TPU:67, one launch (start us, length us, event | category | flops | bytes accessed | tf_op | source)
XLA Modules:
  0.0 165.5 jit_solution(18043006639418743032)
XLA Ops:
  7.7 2.6 %collective-permute-start = (bf16[256,256]{0,1:T(8,128)(2,1)S(1)}, bf16[256,256]{0,1:T(8,128)(2,1)S(1)}, u32[]{:S(2)}, u32[]{:S(2)}) collective-permute-start(bf16[256,256]{0,1:T(8,128)(2,1)S(1)} %get-tuple-element.10), channel_id=1, source_target_pairs={{4,0},{8,4},{12,8},{16,12},{20,16},{24,20},{28,24},{32,28},{36,32}... | collective-permute-start | bytes 393224 | tf_op jit(solution)/shard_map/ppermute | solution.py:23
  10.2 2.7 %collective-permute-start.5 = (bf16[256,256]{0,1:T(8,128)(2,1)S(1)}, bf16[256,256]{0,1:T(8,128)(2,1)S(1)}, u32[]{:S(2)}, u32[]{:S(2)}) collective-permute-start(bf16[256,256]{0,1:T(8,128)(2,1)S(1)} %get-tuple-element.10), channel_id=1, source_target_pairs={{24,0},{28,4},{32,8},{36,12},{40,16},{44,20},{48,24},{52,28},{56,3... | collective-permute-start | bytes 393224 | tf_op jit(solution)/shard_map/ppermute | solution.py:23
  13.0 4.4 %collective-permute-start.4 = (bf16[256,256]{0,1:T(8,128)(2,1)S(1)}, bf16[256,256]{0,1:T(8,128)(2,1)S(1)}, u32[]{:S(2)}, u32[]{:S(2)}) collective-permute-start(bf16[256,256]{0,1:T(8,128)(2,1)S(1)} %get-tuple-element.10), channel_id=1, source_target_pairs={{20,0},{24,4},{28,8},{32,12},{36,16},{40,20},{44,24},{48,28},{52,3... | collective-permute-start | bytes 393224 | tf_op jit(solution)/shard_map/ppermute | solution.py:23
  17.4 3.0 %collective-permute-start.3 = (bf16[256,256]{0,1:T(8,128)(2,1)S(1)}, bf16[256,256]{0,1:T(8,128)(2,1)S(1)}, u32[]{:S(2)}, u32[]{:S(2)}) collective-permute-start(bf16[256,256]{0,1:T(8,128)(2,1)S(1)} %get-tuple-element.10), channel_id=1, source_target_pairs={{16,0},{20,4},{24,8},{28,12},{32,16},{36,20},{40,24},{44,28},{48,3... | collective-permute-start | bytes 393224 | tf_op jit(solution)/shard_map/ppermute | solution.py:23
  20.4 2.0 %collective-permute-start.2 = (bf16[256,256]{0,1:T(8,128)(2,1)S(1)}, bf16[256,256]{0,1:T(8,128)(2,1)S(1)}, u32[]{:S(2)}, u32[]{:S(2)}) collective-permute-start(bf16[256,256]{0,1:T(8,128)(2,1)S(1)} %get-tuple-element.10), channel_id=1, source_target_pairs={{12,0},{16,4},{20,8},{24,12},{28,16},{32,20},{36,24},{40,28},{44,3... | collective-permute-start | bytes 393224 | tf_op jit(solution)/shard_map/ppermute | solution.py:23
  23.4 4.3 %all-to-all-start = ((bf16[4,256,256]{2,1,0:T(8,128)(2,1)}), bf16[4,256,256]{2,1,0:T(8,128)(2,1)S(1)}, u32[]{:S(2)}, u32[]{:S(2)}) async-start(bf16[4,256,256]{2,1,0:T(8,128)(2,1)} %tile.8), calls=%async_computation.1 | async-start | bytes 1048576 | tf_op jit(solution)/shard_map/all_to_all | solution.py:14
  28.3 6.1 %copy.15 = bf16[1,1024,7,256]{1,3,2,0:T(8,128)(2,1)} copy(bf16[1,1024,7,256]{3,1,2,0:T(8,128)(2,1)} %param.5) | data formatting | bytes 7340032 | tf_op args[0]
  34.5 6.4 %collective-permute-start.1 = (bf16[256,256]{0,1:T(8,128)(2,1)S(1)}, bf16[256,256]{0,1:T(8,128)(2,1)S(1)}, u32[]{:S(2)}, u32[]{:S(2)}) collective-permute-start(bf16[256,256]{0,1:T(8,128)(2,1)S(1)} %get-tuple-element.10), channel_id=1, source_target_pairs={{8,0},{12,4},{16,8},{20,12},{24,16},{28,20},{32,24},{36,28},{40,32... | collective-permute-start | bytes 393224 | tf_op jit(solution)/shard_map/ppermute | solution.py:23
  40.9 3.8 %collective-permute-done.1 = bf16[256,256]{0,1:T(8,128)(2,1)S(1)} collective-permute-done((bf16[256,256]{0,1:T(8,128)(2,1)S(1)}, bf16[256,256]{0,1:T(8,128)(2,1)S(1)}, u32[]{:S(2)}, u32[]{:S(2)}) %collective-permute-start.1) | collective-permute-done | bytes 131104 | tf_op jit(solution)/shard_map/ppermute | solution.py:23
  45.7 4.0 %fusion.5 = bf16[1024,256]{0,1:T(8,128)(2,1)} fusion(bf16[1792,256]{1,0:T(8,128)(2,1)S(1)} %bitcast.150, bf16[1024,1792]{0,1:T(8,128)(2,1)} %bitcast.145), kind=kOutput, calls=%fused_computation.6 | convolution fusion | flops 939786240 | bytes 5111808 | tf_op jit(solution)/shard_map/dot_general | solution.py:55
  49.7 3.2 %fusion.28 = (bf16[7,256,256]{1,2,0:T(8,128)(2,1)S(1)}, f32[7,256,256]{1,2,0:T(8,128)S(1)}) fusion(f32[7]{0:T(128)S(1)} %compare_convert_fusion, bf16[1024,256,1]{1,0,2:T(8,128)(2,1)S(1)} %bitcast.149, bf16[1,1024,7,256]{1,3,2,0:T(8,128)(2,1)} %copy.15), kind=kOutput, calls=%fused_computation.67 | convolution fusion | flops 940441600 | bytes 6946844 | tf_op jit(solution)/shard_map/dot_general | solution.py:63
  53.0 4.5 %collective-permute-start.6 = (bf16[256,256]{0,1:T(8,128)(2,1)S(1)}, bf16[256,256]{0,1:T(8,128)(2,1)S(1)}, u32[]{:S(2)}, u32[]{:S(2)}) collective-permute-start(bf16[256,256]{0,1:T(8,128)(2,1)S(1)} %get-tuple-element.17), channel_id=1, source_target_pairs={{0,4},{4,8},{8,12},{12,16},{16,20},{20,24},{24,28},{28,32},{32,36}... | collective-permute-start | bytes 393224 | tf_op jit(solution)/shard_map/ppermute | solution.py:23
  57.5 2.1 %collective-permute-start.11 = (bf16[256,256]{0,1:T(8,128)(2,1)S(1)}, bf16[256,256]{0,1:T(8,128)(2,1)S(1)}, u32[]{:S(2)}, u32[]{:S(2)}) collective-permute-start(bf16[256,256]{0,1:T(8,128)(2,1)S(1)} %get-tuple-element.18), channel_id=1, source_target_pairs={{0,24},{4,28},{8,32},{12,36},{16,40},{20,44},{24,48},{28,52},{32,5... | collective-permute-start | bytes 393224 | tf_op jit(solution)/shard_map/ppermute | solution.py:23
  61.5 5.3 %collective-permute-start.9 = (bf16[256,256]{0,1:T(8,128)(2,1)S(1)}, bf16[256,256]{0,1:T(8,128)(2,1)S(1)}, u32[]{:S(2)}, u32[]{:S(2)}) collective-permute-start(bf16[256,256]{0,1:T(8,128)(2,1)S(1)} %get-tuple-element.20), channel_id=1, source_target_pairs={{0,16},{4,20},{8,24},{12,28},{16,32},{20,36},{24,40},{28,44},{32,4... | collective-permute-start | bytes 393224 | tf_op jit(solution)/shard_map/ppermute | solution.py:23
  66.9 5.3 %collective-permute-start.8 = (bf16[256,256]{0,1:T(8,128)(2,1)S(1)}, bf16[256,256]{0,1:T(8,128)(2,1)S(1)}, u32[]{:S(2)}, u32[]{:S(2)}) collective-permute-start(bf16[256,256]{0,1:T(8,128)(2,1)S(1)} %get-tuple-element.21), channel_id=1, source_target_pairs={{0,12},{4,16},{8,20},{12,24},{16,28},{20,32},{24,36},{28,40},{32,4... | collective-permute-start | bytes 393224 | tf_op jit(solution)/shard_map/ppermute | solution.py:23
  72.2 4.1 %collective-permute-start.7 = (bf16[256,256]{0,1:T(8,128)(2,1)S(1)}, bf16[256,256]{0,1:T(8,128)(2,1)S(1)}, u32[]{:S(2)}, u32[]{:S(2)}) collective-permute-start(bf16[256,256]{0,1:T(8,128)(2,1)S(1)} %get-tuple-element.22), channel_id=1, source_target_pairs={{0,8},{4,12},{8,16},{12,20},{16,24},{20,28},{24,32},{28,36},{32,40... | collective-permute-start | bytes 393224 | tf_op jit(solution)/shard_map/ppermute | solution.py:23
  76.5 4.9 %collective-permute-done.7 = bf16[256,256]{0,1:T(8,128)(2,1)S(1)} collective-permute-done((bf16[256,256]{0,1:T(8,128)(2,1)S(1)}, bf16[256,256]{0,1:T(8,128)(2,1)S(1)}, u32[]{:S(2)}, u32[]{:S(2)}) %collective-permute-start.7) | collective-permute-done | bytes 131104 | tf_op jit(solution)/shard_map/ppermute | solution.py:23
  83.6 2.3 %collective-permute-start.12 = (bf16[256,256]{0,1:T(8,128)(2,1)S(1)}, bf16[256,256]{0,1:T(8,128)(2,1)S(1)}, u32[]{:S(2)}, u32[]{:S(2)}) collective-permute-start(bf16[256,256]{0,1:T(8,128)(2,1)S(1)} %get-tuple-element.6), channel_id=1, source_target_pairs={{4,0},{8,4},{12,8},{16,12},{20,16},{24,20},{28,24},{32,28},{36,32}... | collective-permute-start | bytes 393224 | tf_op jit(solution)/shard_map/ppermute | solution.py:23
  86.0 2.6 %collective-permute-start.17 = (bf16[256,256]{0,1:T(8,128)(2,1)S(1)}, bf16[256,256]{0,1:T(8,128)(2,1)S(1)}, u32[]{:S(2)}, u32[]{:S(2)}) collective-permute-start(bf16[256,256]{0,1:T(8,128)(2,1)S(1)} %get-tuple-element.6), channel_id=1, source_target_pairs={{24,0},{28,4},{32,8},{36,12},{40,16},{44,20},{48,24},{52,28},{56,3... | collective-permute-start | bytes 393224 | tf_op jit(solution)/shard_map/ppermute | solution.py:23
  88.5 4.5 %collective-permute-start.16 = (bf16[256,256]{0,1:T(8,128)(2,1)S(1)}, bf16[256,256]{0,1:T(8,128)(2,1)S(1)}, u32[]{:S(2)}, u32[]{:S(2)}) collective-permute-start(bf16[256,256]{0,1:T(8,128)(2,1)S(1)} %get-tuple-element.6), channel_id=1, source_target_pairs={{20,0},{24,4},{28,8},{32,12},{36,16},{40,20},{44,24},{48,28},{52,3... | collective-permute-start | bytes 393224 | tf_op jit(solution)/shard_map/ppermute | solution.py:23
  93.0 2.4 %collective-permute-start.15 = (bf16[256,256]{0,1:T(8,128)(2,1)S(1)}, bf16[256,256]{0,1:T(8,128)(2,1)S(1)}, u32[]{:S(2)}, u32[]{:S(2)}) collective-permute-start(bf16[256,256]{0,1:T(8,128)(2,1)S(1)} %get-tuple-element.6), channel_id=1, source_target_pairs={{16,0},{20,4},{24,8},{28,12},{32,16},{36,20},{40,24},{44,28},{48,3... | collective-permute-start | bytes 393224 | tf_op jit(solution)/shard_map/ppermute | solution.py:23
  95.4 2.8 %collective-permute-start.14 = (bf16[256,256]{0,1:T(8,128)(2,1)S(1)}, bf16[256,256]{0,1:T(8,128)(2,1)S(1)}, u32[]{:S(2)}, u32[]{:S(2)}) collective-permute-start(bf16[256,256]{0,1:T(8,128)(2,1)S(1)} %get-tuple-element.6), channel_id=1, source_target_pairs={{12,0},{16,4},{20,8},{24,12},{28,16},{32,20},{36,24},{40,28},{44,3... | collective-permute-start | bytes 393224 | tf_op jit(solution)/shard_map/ppermute | solution.py:23
  99.2 6.5 %all-to-all-start.1 = ((bf16[4,256,256]{2,1,0:T(8,128)(2,1)}), bf16[4,256,256]{2,1,0:T(8,128)(2,1)}, u32[]{:S(2)}, u32[]{:S(2)}) async-start(bf16[4,256,256]{2,1,0:T(8,128)(2,1)} %tile.11), calls=%async_computation.3 | async-start | bytes 1048576 | tf_op jit(solution)/shard_map/all_to_all | solution.py:14
  107.6 4.6 %collective-permute-done.13 = bf16[256,256]{0,1:T(8,128)(2,1)S(1)} collective-permute-done((bf16[256,256]{0,1:T(8,128)(2,1)S(1)}, bf16[256,256]{0,1:T(8,128)(2,1)S(1)}, u32[]{:S(2)}, u32[]{:S(2)}) %collective-permute-start.13) | collective-permute-done | bytes 131104 | tf_op jit(solution)/shard_map/ppermute | solution.py:23
  113.1 4.0 %fusion.6 = bf16[1024,256]{0,1:T(8,128)(2,1)} fusion(bf16[1792,256]{1,0:T(8,128)(2,1)S(1)} %bitcast.151, bf16[1024,1792]{0,1:T(8,128)(2,1)} %bitcast.146), kind=kOutput, calls=%fused_computation.7 | convolution fusion | flops 939786240 | bytes 5111808 | tf_op jit(solution)/shard_map/dot_general | solution.py:55
  117.2 3.4 %convolution_bitcast_fusion = f32[1792,256]{0,1:T(8,128)S(1)} fusion(bf16[1024,256]{1,0:T(8,128)(2,1)} %bitcast.32, bf16[1024,1792]{0,1:T(8,128)(2,1)} %bitcast.147), kind=kOutput, calls=%fused_computation.2 | convolution fusion | flops 939524096 | bytes 6029312 | tf_op jit(solution)/shard_map/dot_general | solution.py:63
  125.7 3.6 %collective-permute-start.18 = (bf16[256,256]{0,1:T(8,128)(2,1)S(1)}, bf16[256,256]{0,1:T(8,128)(2,1)S(1)}, u32[]{:S(2)}, u32[]{:S(2)}) collective-permute-start(bf16[256,256]{0,1:T(8,128)(2,1)S(1)} %get-tuple-element.11), channel_id=1, source_target_pairs={{0,4},{4,8},{8,12},{12,16},{16,20},{20,24},{24,28},{28,32},{32,36}... | collective-permute-start | bytes 393224 | tf_op jit(solution)/shard_map/ppermute | solution.py:23
  129.2 6.1 %collective-permute-start.23 = (bf16[256,256]{0,1:T(8,128)(2,1)S(1)}, bf16[256,256]{0,1:T(8,128)(2,1)S(1)}, u32[]{:S(2)}, u32[]{:S(2)}) collective-permute-start(bf16[256,256]{0,1:T(8,128)(2,1)S(1)} %get-tuple-element.12), channel_id=1, source_target_pairs={{0,24},{4,28},{8,32},{12,36},{16,40},{20,44},{24,48},{28,52},{32,5... | collective-permute-start | bytes 393224 | tf_op jit(solution)/shard_map/ppermute | solution.py:23
  137.3 4.9 %collective-permute-start.21 = (bf16[256,256]{0,1:T(8,128)(2,1)S(1)}, bf16[256,256]{0,1:T(8,128)(2,1)S(1)}, u32[]{:S(2)}, u32[]{:S(2)}) collective-permute-start(bf16[256,256]{0,1:T(8,128)(2,1)S(1)} %get-tuple-element.14), channel_id=1, source_target_pairs={{0,16},{4,20},{8,24},{12,28},{16,32},{20,36},{24,40},{28,44},{32,4... | collective-permute-start | bytes 393224 | tf_op jit(solution)/shard_map/ppermute | solution.py:23
  142.1 5.7 %collective-permute-start.20 = (bf16[256,256]{0,1:T(8,128)(2,1)S(1)}, bf16[256,256]{0,1:T(8,128)(2,1)S(1)}, u32[]{:S(2)}, u32[]{:S(2)}) collective-permute-start(bf16[256,256]{0,1:T(8,128)(2,1)S(1)} %get-tuple-element.15), channel_id=1, source_target_pairs={{0,12},{4,16},{8,20},{12,24},{16,28},{20,32},{24,36},{28,40},{32,4... | collective-permute-start | bytes 393224 | tf_op jit(solution)/shard_map/ppermute | solution.py:23
  147.8 3.6 %collective-permute-start.19 = (bf16[256,256]{0,1:T(8,128)(2,1)S(1)}, bf16[256,256]{0,1:T(8,128)(2,1)S(1)}, u32[]{:S(2)}, u32[]{:S(2)}) collective-permute-start(bf16[256,256]{0,1:T(8,128)(2,1)S(1)} %get-tuple-element.16), channel_id=1, source_target_pairs={{0,8},{4,12},{8,16},{12,20},{16,24},{20,28},{24,32},{28,36},{32,40... | collective-permute-start | bytes 393224 | tf_op jit(solution)/shard_map/ppermute | solution.py:23
  153.5 3.0 %collective-permute-done.19 = bf16[256,256]{0,1:T(8,128)(2,1)S(1)} collective-permute-done((bf16[256,256]{0,1:T(8,128)(2,1)S(1)}, bf16[256,256]{0,1:T(8,128)(2,1)S(1)}, u32[]{:S(2)}, u32[]{:S(2)}) %collective-permute-start.19) | collective-permute-done | bytes 131104 | tf_op jit(solution)/shard_map/ppermute | solution.py:23
  (80 shorter events, 21.9 us)
Async XLA Ops:
  7.7 26.8 %collective-permute-start = (bf16[256,256]{0,1:T(8,128)(2,1)S(1)}, bf16[256,256]{0,1:T(8,128)(2,1)S(1)}, u32[]{:S(2)}, u32[]{:S(2)}) collective-permute-start(bf16[256,256]{0,1:T(8,128)(2,1)S(1)} %get-tuple-element.10), channel_id=1, source_target_pairs={{4,0},{8,4},{12,8},{16,12},{20,16},{24,20},{28,24},{32,28},{36,32}... | collective-permute-start | bytes 393224 | tf_op jit(solution)/shard_map/ppermute | solution.py:23
  10.2 34.6 %collective-permute-start.5 = (bf16[256,256]{0,1:T(8,128)(2,1)S(1)}, bf16[256,256]{0,1:T(8,128)(2,1)S(1)}, u32[]{:S(2)}, u32[]{:S(2)}) collective-permute-start(bf16[256,256]{0,1:T(8,128)(2,1)S(1)} %get-tuple-element.10), channel_id=1, source_target_pairs={{24,0},{28,4},{32,8},{36,12},{40,16},{44,20},{48,24},{52,28},{56,3... | collective-permute-start | bytes 393224 | tf_op jit(solution)/shard_map/ppermute | solution.py:23
  13.0 31.8 %collective-permute-start.4 = (bf16[256,256]{0,1:T(8,128)(2,1)S(1)}, bf16[256,256]{0,1:T(8,128)(2,1)S(1)}, u32[]{:S(2)}, u32[]{:S(2)}) collective-permute-start(bf16[256,256]{0,1:T(8,128)(2,1)S(1)} %get-tuple-element.10), channel_id=1, source_target_pairs={{20,0},{24,4},{28,8},{32,12},{36,16},{40,20},{44,24},{48,28},{52,3... | collective-permute-start | bytes 393224 | tf_op jit(solution)/shard_map/ppermute | solution.py:23
  17.4 27.4 %collective-permute-start.3 = (bf16[256,256]{0,1:T(8,128)(2,1)S(1)}, bf16[256,256]{0,1:T(8,128)(2,1)S(1)}, u32[]{:S(2)}, u32[]{:S(2)}) collective-permute-start(bf16[256,256]{0,1:T(8,128)(2,1)S(1)} %get-tuple-element.10), channel_id=1, source_target_pairs={{16,0},{20,4},{24,8},{28,12},{32,16},{36,20},{40,24},{44,28},{48,3... | collective-permute-start | bytes 393224 | tf_op jit(solution)/shard_map/ppermute | solution.py:23
  20.4 24.4 %collective-permute-start.2 = (bf16[256,256]{0,1:T(8,128)(2,1)S(1)}, bf16[256,256]{0,1:T(8,128)(2,1)S(1)}, u32[]{:S(2)}, u32[]{:S(2)}) collective-permute-start(bf16[256,256]{0,1:T(8,128)(2,1)S(1)} %get-tuple-element.10), channel_id=1, source_target_pairs={{12,0},{16,4},{20,8},{24,12},{28,16},{32,20},{36,24},{40,28},{44,3... | collective-permute-start | bytes 393224 | tf_op jit(solution)/shard_map/ppermute | solution.py:23
  23.4 26.3 %all-to-all-start = ((bf16[4,256,256]{2,1,0:T(8,128)(2,1)}), bf16[4,256,256]{2,1,0:T(8,128)(2,1)S(1)}, u32[]{:S(2)}, u32[]{:S(2)}) async-start(bf16[4,256,256]{2,1,0:T(8,128)(2,1)} %tile.8), calls=%async_computation.1 | async-start | bytes 1048576 | tf_op jit(solution)/shard_map/all_to_all | solution.py:14
  27.7 53.7 %reduce-scatter.3.cloned.1.call-start = ((), (), s32[]{:S(2)}) async-start(), calls=%async_computation.4 | async-start | bytes 655360 | tf_op jit(solution)/shard_map/reduce_scatter | solution.py:57
  34.5 10.3 %collective-permute-start.1 = (bf16[256,256]{0,1:T(8,128)(2,1)S(1)}, bf16[256,256]{0,1:T(8,128)(2,1)S(1)}, u32[]{:S(2)}, u32[]{:S(2)}) collective-permute-start(bf16[256,256]{0,1:T(8,128)(2,1)S(1)} %get-tuple-element.10), channel_id=1, source_target_pairs={{8,0},{12,4},{16,8},{20,12},{24,16},{28,20},{32,24},{36,28},{40,32... | collective-permute-start | bytes 393224 | tf_op jit(solution)/shard_map/ppermute | solution.py:23
  49.7 26.7 %copy-start.7 = (f32[256]{0:T(256)S(1)}, f32[256]{0:T(256)}, u32[]{:S(2)}) copy-start(f32[256]{0:T(256)} %param.9) | copy-start | bytes 3076
  49.7 32.3 %copy-start = (f32[256,64]{0,1:T(8,128)S(1)}, f32[256,64]{0,1:T(8,128)}, u32[]{:S(2)}) copy-start(f32[256,64]{0,1:T(8,128)} %param.8) | copy-start | bytes 196612
  53.0 19.2 %collective-permute-start.6 = (bf16[256,256]{0,1:T(8,128)(2,1)S(1)}, bf16[256,256]{0,1:T(8,128)(2,1)S(1)}, u32[]{:S(2)}, u32[]{:S(2)}) collective-permute-start(bf16[256,256]{0,1:T(8,128)(2,1)S(1)} %get-tuple-element.17), channel_id=1, source_target_pairs={{0,4},{4,8},{8,12},{12,16},{16,20},{20,24},{24,28},{28,32},{32,36}... | collective-permute-start | bytes 393224 | tf_op jit(solution)/shard_map/ppermute | solution.py:23
  57.5 18.9 %collective-permute-start.11 = (bf16[256,256]{0,1:T(8,128)(2,1)S(1)}, bf16[256,256]{0,1:T(8,128)(2,1)S(1)}, u32[]{:S(2)}, u32[]{:S(2)}) collective-permute-start(bf16[256,256]{0,1:T(8,128)(2,1)S(1)} %get-tuple-element.18), channel_id=1, source_target_pairs={{0,24},{4,28},{8,32},{12,36},{16,40},{20,44},{24,48},{28,52},{32,5... | collective-permute-start | bytes 393224 | tf_op jit(solution)/shard_map/ppermute | solution.py:23
  59.6 16.8 %collective-permute-start.10 = (bf16[256,256]{0,1:T(8,128)(2,1)S(1)}, bf16[256,256]{0,1:T(8,128)(2,1)S(1)}, u32[]{:S(2)}, u32[]{:S(2)}) collective-permute-start(bf16[256,256]{0,1:T(8,128)(2,1)S(1)} %get-tuple-element.19), channel_id=1, source_target_pairs={{0,20},{4,24},{8,28},{12,32},{16,36},{20,40},{24,44},{28,48},{32,5... | collective-permute-start | bytes 393224 | tf_op jit(solution)/shard_map/ppermute | solution.py:23
  61.5 14.9 %collective-permute-start.9 = (bf16[256,256]{0,1:T(8,128)(2,1)S(1)}, bf16[256,256]{0,1:T(8,128)(2,1)S(1)}, u32[]{:S(2)}, u32[]{:S(2)}) collective-permute-start(bf16[256,256]{0,1:T(8,128)(2,1)S(1)} %get-tuple-element.20), channel_id=1, source_target_pairs={{0,16},{4,20},{8,24},{12,28},{16,32},{20,36},{24,40},{28,44},{32,4... | collective-permute-start | bytes 393224 | tf_op jit(solution)/shard_map/ppermute | solution.py:23
  66.9 9.6 %collective-permute-start.8 = (bf16[256,256]{0,1:T(8,128)(2,1)S(1)}, bf16[256,256]{0,1:T(8,128)(2,1)S(1)}, u32[]{:S(2)}, u32[]{:S(2)}) collective-permute-start(bf16[256,256]{0,1:T(8,128)(2,1)S(1)} %get-tuple-element.21), channel_id=1, source_target_pairs={{0,12},{4,16},{8,20},{12,24},{16,28},{20,32},{24,36},{28,40},{32,4... | collective-permute-start | bytes 393224 | tf_op jit(solution)/shard_map/ppermute | solution.py:23
  72.2 9.2 %copy-start.1 = (bf16[256,256]{0,1:T(8,128)(2,1)}, bf16[256,256]{0,1:T(8,128)(2,1)S(1)}, u32[]{:S(2)}) copy-start(bf16[256,256]{0,1:T(8,128)(2,1)S(1)} %collective-permute-done.6) | copy-start | bytes 393220
  72.2 9.1 %collective-permute-start.7 = (bf16[256,256]{0,1:T(8,128)(2,1)S(1)}, bf16[256,256]{0,1:T(8,128)(2,1)S(1)}, u32[]{:S(2)}, u32[]{:S(2)}) collective-permute-start(bf16[256,256]{0,1:T(8,128)(2,1)S(1)} %get-tuple-element.22), channel_id=1, source_target_pairs={{0,8},{4,12},{8,16},{12,20},{16,24},{20,28},{24,32},{28,36},{32,40... | collective-permute-start | bytes 393224 | tf_op jit(solution)/shard_map/ppermute | solution.py:23
  76.4 5.0 %copy-start.2 = (bf16[256,256]{0,1:T(8,128)(2,1)}, bf16[256,256]{0,1:T(8,128)(2,1)S(1)}, u32[]{:S(2)}) copy-start(bf16[256,256]{0,1:T(8,128)(2,1)S(1)} %collective-permute-done.11) | copy-start | bytes 393220
  83.6 22.1 %collective-permute-start.12 = (bf16[256,256]{0,1:T(8,128)(2,1)S(1)}, bf16[256,256]{0,1:T(8,128)(2,1)S(1)}, u32[]{:S(2)}, u32[]{:S(2)}) collective-permute-start(bf16[256,256]{0,1:T(8,128)(2,1)S(1)} %get-tuple-element.6), channel_id=1, source_target_pairs={{4,0},{8,4},{12,8},{16,12},{20,16},{24,20},{28,24},{32,28},{36,32}... | collective-permute-start | bytes 393224 | tf_op jit(solution)/shard_map/ppermute | solution.py:23
  86.0 26.4 %collective-permute-start.17 = (bf16[256,256]{0,1:T(8,128)(2,1)S(1)}, bf16[256,256]{0,1:T(8,128)(2,1)S(1)}, u32[]{:S(2)}, u32[]{:S(2)}) collective-permute-start(bf16[256,256]{0,1:T(8,128)(2,1)S(1)} %get-tuple-element.6), channel_id=1, source_target_pairs={{24,0},{28,4},{32,8},{36,12},{40,16},{44,20},{48,24},{52,28},{56,3... | collective-permute-start | bytes 393224 | tf_op jit(solution)/shard_map/ppermute | solution.py:23
  88.5 23.8 %collective-permute-start.16 = (bf16[256,256]{0,1:T(8,128)(2,1)S(1)}, bf16[256,256]{0,1:T(8,128)(2,1)S(1)}, u32[]{:S(2)}, u32[]{:S(2)}) collective-permute-start(bf16[256,256]{0,1:T(8,128)(2,1)S(1)} %get-tuple-element.6), channel_id=1, source_target_pairs={{20,0},{24,4},{28,8},{32,12},{36,16},{40,20},{44,24},{48,28},{52,3... | collective-permute-start | bytes 393224 | tf_op jit(solution)/shard_map/ppermute | solution.py:23
  93.0 19.3 %collective-permute-start.15 = (bf16[256,256]{0,1:T(8,128)(2,1)S(1)}, bf16[256,256]{0,1:T(8,128)(2,1)S(1)}, u32[]{:S(2)}, u32[]{:S(2)}) collective-permute-start(bf16[256,256]{0,1:T(8,128)(2,1)S(1)} %get-tuple-element.6), channel_id=1, source_target_pairs={{16,0},{20,4},{24,8},{28,12},{32,16},{36,20},{40,24},{44,28},{48,3... | collective-permute-start | bytes 393224 | tf_op jit(solution)/shard_map/ppermute | solution.py:23
  95.4 16.8 %collective-permute-start.14 = (bf16[256,256]{0,1:T(8,128)(2,1)S(1)}, bf16[256,256]{0,1:T(8,128)(2,1)S(1)}, u32[]{:S(2)}, u32[]{:S(2)}) collective-permute-start(bf16[256,256]{0,1:T(8,128)(2,1)S(1)} %get-tuple-element.6), channel_id=1, source_target_pairs={{12,0},{16,4},{20,8},{24,12},{28,16},{32,20},{36,24},{40,28},{44,3... | collective-permute-start | bytes 393224 | tf_op jit(solution)/shard_map/ppermute | solution.py:23
  99.2 18.0 %all-to-all-start.1 = ((bf16[4,256,256]{2,1,0:T(8,128)(2,1)}), bf16[4,256,256]{2,1,0:T(8,128)(2,1)}, u32[]{:S(2)}, u32[]{:S(2)}) async-start(bf16[4,256,256]{2,1,0:T(8,128)(2,1)} %tile.11), calls=%async_computation.3 | async-start | bytes 1048576 | tf_op jit(solution)/shard_map/all_to_all | solution.py:14
  105.7 50.9 %reduce-scatter.5.cloned.1.call-start = ((), (), s32[]{:S(2)}) async-start(), calls=%async_computation.5 | async-start | bytes 655360 | tf_op jit(solution)/shard_map/reduce_scatter | solution.py:57
  105.7 6.5 %collective-permute-start.13 = (bf16[256,256]{0,1:T(8,128)(2,1)S(1)}, bf16[256,256]{0,1:T(8,128)(2,1)S(1)}, u32[]{:S(2)}, u32[]{:S(2)}) collective-permute-start(bf16[256,256]{0,1:T(8,128)(2,1)S(1)} %get-tuple-element.6), channel_id=1, source_target_pairs={{8,0},{12,4},{16,8},{20,12},{24,16},{28,20},{32,24},{36,28},{40,32... | collective-permute-start | bytes 393224 | tf_op jit(solution)/shard_map/ppermute | solution.py:23
  125.7 22.2 %collective-permute-start.18 = (bf16[256,256]{0,1:T(8,128)(2,1)S(1)}, bf16[256,256]{0,1:T(8,128)(2,1)S(1)}, u32[]{:S(2)}, u32[]{:S(2)}) collective-permute-start(bf16[256,256]{0,1:T(8,128)(2,1)S(1)} %get-tuple-element.11), channel_id=1, source_target_pairs={{0,4},{4,8},{8,12},{12,16},{16,20},{20,24},{24,28},{28,32},{32,36}... | collective-permute-start | bytes 393224 | tf_op jit(solution)/shard_map/ppermute | solution.py:23
  129.2 22.2 %collective-permute-start.23 = (bf16[256,256]{0,1:T(8,128)(2,1)S(1)}, bf16[256,256]{0,1:T(8,128)(2,1)S(1)}, u32[]{:S(2)}, u32[]{:S(2)}) collective-permute-start(bf16[256,256]{0,1:T(8,128)(2,1)S(1)} %get-tuple-element.12), channel_id=1, source_target_pairs={{0,24},{4,28},{8,32},{12,36},{16,40},{20,44},{24,48},{28,52},{32,5... | collective-permute-start | bytes 393224 | tf_op jit(solution)/shard_map/ppermute | solution.py:23
  135.3 16.1 %collective-permute-start.22 = (bf16[256,256]{0,1:T(8,128)(2,1)S(1)}, bf16[256,256]{0,1:T(8,128)(2,1)S(1)}, u32[]{:S(2)}, u32[]{:S(2)}) collective-permute-start(bf16[256,256]{0,1:T(8,128)(2,1)S(1)} %get-tuple-element.13), channel_id=1, source_target_pairs={{0,20},{4,24},{8,28},{12,32},{16,36},{20,40},{24,44},{28,48},{32,5... | collective-permute-start | bytes 393224 | tf_op jit(solution)/shard_map/ppermute | solution.py:23
  137.3 14.2 %collective-permute-start.21 = (bf16[256,256]{0,1:T(8,128)(2,1)S(1)}, bf16[256,256]{0,1:T(8,128)(2,1)S(1)}, u32[]{:S(2)}, u32[]{:S(2)}) collective-permute-start(bf16[256,256]{0,1:T(8,128)(2,1)S(1)} %get-tuple-element.14), channel_id=1, source_target_pairs={{0,16},{4,20},{8,24},{12,28},{16,32},{20,36},{24,40},{28,44},{32,4... | collective-permute-start | bytes 393224 | tf_op jit(solution)/shard_map/ppermute | solution.py:23
  142.1 11.4 %collective-permute-start.20 = (bf16[256,256]{0,1:T(8,128)(2,1)S(1)}, bf16[256,256]{0,1:T(8,128)(2,1)S(1)}, u32[]{:S(2)}, u32[]{:S(2)}) collective-permute-start(bf16[256,256]{0,1:T(8,128)(2,1)S(1)} %get-tuple-element.15), channel_id=1, source_target_pairs={{0,12},{4,16},{8,20},{12,24},{16,28},{20,32},{24,36},{28,40},{32,4... | collective-permute-start | bytes 393224 | tf_op jit(solution)/shard_map/ppermute | solution.py:23
  147.8 8.7 %collective-permute-start.19 = (bf16[256,256]{0,1:T(8,128)(2,1)S(1)}, bf16[256,256]{0,1:T(8,128)(2,1)S(1)}, u32[]{:S(2)}, u32[]{:S(2)}) collective-permute-start(bf16[256,256]{0,1:T(8,128)(2,1)S(1)} %get-tuple-element.16), channel_id=1, source_target_pairs={{0,8},{4,12},{8,16},{12,20},{16,24},{20,28},{24,32},{28,36},{32,40... | collective-permute-start | bytes 393224 | tf_op jit(solution)/shard_map/ppermute | solution.py:23
  (4 other events, 15.6 us)
Sparse Core Ops, SparseCore 0:
  49.8 29.9 reduce-scatter.2
  117.3 30.0 reduce-scatter.4
